TPU v7x, 512 devices: a whole 4x8x8 slice. The times are simulated.
512 devices in a mesh: seq: 32 (over y_hi, z, core), chan: 16 (over x, y_lo).
Axes of the slice: x: 4, y: 8 (y_hi: 2, y_lo: 4; y = y_hi * 4 + y_lo), z: 8, core: 2. Of those that a mesh axis runs over, the one named last changes fastest.
Arguments:
- values: bfloat16 [4096, 1024], P('seq', 'chan'), may hold values from -6 to 6
- gate_inner: bfloat16 [4096, 1024], P('seq', 'chan'), may hold values from -6 to 6
- gate_outer: bfloat16 [4096, 1024], P('seq', 'chan'), may hold values from -6 to 6
- filter_one: float32 [16, 4096], P('chan', 'seq'), may hold values from -0.09375 to 0.09375
- filter_two: float32 [16, 4096], P('chan', 'seq'), may hold values from -0.09375 to 0.09375
- teacher: bfloat16 [4096, 1024], P('seq', 'chan'), may hold values from -6 to 6
- w_out: bfloat16 [1024, 1024], P(None, 'chan'), may hold values from -0.1875 to 0.1875
- gene_ids: int32 [4096], P('seq'), may hold values from 0 to 25425
- cell_lengths: int32 [4], replicated, may hold values from 1 to 2048, 4096 in all
- gene_weights: float32 [25426], replicated, may hold values from 0.5 to 2
Outputs:
- grad_values: bfloat16 [4096, 1024], P('seq', 'chan')
- grad_inner: bfloat16 [4096, 1024], P('seq', 'chan')
- grad_outer: bfloat16 [4096, 1024], P('seq', 'chan')
- grad_filter_one: float32 [16, 4096], P('chan', 'seq')
- grad_filter_two: float32 [16, 4096], P('chan', 'seq')
- grad_w_out: float32 [1024, 1024], P('seq', 'chan')
Inputs may be any that keep to these rules, and one draw needn't show every extreme that they name: `cell_lengths`: the lengths sum to 4096, and the largest equals 2048.
All inputs are finite; a program needn't handle non-finite values.
Results may differ from a plain program's by a relative error of at most 0.0051.
Values may be sent and summed in bfloat16 or wider, within the bound.
A program may use at most 64 MiB of HBM per device.

v0:
```python
import jax
import jax.numpy as jnp
from jax import lax
from jax.sharding import PartitionSpec as P

TWO_PI = 6.283185307179586
PRECISE = lax.Precision.HIGHEST


def phases(left_index, right_index, modulus):
    turn_count = left_index[:, None] * right_index[None, :] % modulus
    centred = jnp.where(2 * turn_count > modulus, turn_count - modulus, turn_count)
    radians = centred.astype(jnp.float32) * (TWO_PI / modulus)
    return (jnp.cos(radians), jnp.sin(radians))


def make_tables(length, shard_count, position):
    stride = length // shard_count
    lane_index = jnp.arange(shard_count, dtype=jnp.int32)
    doubled = jnp.arange(2 * shard_count, dtype=jnp.int32)
    padded_len = 2 * shard_count * length
    offsets = jnp.arange(length, dtype=jnp.int32)
    wide_cos, wide_sin = phases(lane_index, doubled, 2 * shard_count)
    near_cos, near_sin = phases(
        position * stride + jnp.arange(stride, dtype=jnp.int32), doubled, padded_len
    )
    far_cos, far_sin = phases(offsets, 2 * position + jnp.arange(2, dtype=jnp.int32), padded_len)
    long_cos, long_sin = phases(offsets, offsets, length)
    return (wide_cos, wide_sin, near_cos, near_sin, far_cos, far_sin, long_cos, long_sin)


def spread_out(packed):
    return lax.all_to_all(packed, "seq", split_axis=0, concat_axis=1, tiled=True)


def bring_back(packed):
    return lax.all_to_all(packed, "seq", split_axis=1, concat_axis=0, tiled=True)


def halves(packed):
    half_width = packed.shape[-1] // 2
    return (packed[..., :half_width], packed[..., half_width:])


def long_transform(real_in, imag_in, table_cos, table_sin, sign):
    shape_in = real_in.shape
    stacked = jnp.concatenate(
        [real_in.reshape(shape_in[0], -1), imag_in.reshape(shape_in[0], -1)], axis=1
    )
    cos_part = jnp.dot(table_cos, stacked, precision=PRECISE)
    sin_part = jnp.dot(table_sin, stacked, precision=PRECISE)
    cos_real, cos_imag = halves(cos_part)
    sin_real, sin_imag = halves(sin_part)
    real_out = cos_real + sign * sin_imag
    imag_out = cos_imag - sign * sin_real
    return (real_out.reshape(shape_in), imag_out.reshape(shape_in))


def forward_columns(columns, tables):
    wide_cos, wide_sin, near_cos, near_sin, far_cos, far_sin, long_cos, long_sin = tables
    real_part = jnp.einsum("rnf,nk->rkf", columns, wide_cos, precision=PRECISE)
    imag_part = -jnp.einsum("rnf,nk->rkf", columns, wide_sin, precision=PRECISE)
    twist_cos = near_cos[:, :, None]
    twist_sin = near_sin[:, :, None]
    turned = jnp.concatenate(
        [
            real_part * twist_cos + imag_part * twist_sin,
            imag_part * twist_cos - real_part * twist_sin,
        ],
        axis=2,
    )
    arrived_real, arrived_imag = halves(bring_back(turned))
    return long_transform(arrived_real, arrived_imag, long_cos, long_sin, 1.0)


def inverse_columns(spectra, tables):
    wide_cos, wide_sin, near_cos, near_sin, far_cos, far_sin, long_cos, long_sin = tables
    time_real, time_imag = long_transform(spectra[0], spectra[1], long_cos, long_sin, -1.0)
    twist_cos = far_cos[:, :, None]
    twist_sin = far_sin[:, :, None]
    turned = jnp.concatenate(
        [
            time_real * twist_cos - time_imag * twist_sin,
            time_imag * twist_cos + time_real * twist_sin,
        ],
        axis=2,
    )
    arrived_real, arrived_imag = halves(spread_out(turned))
    padded_len = 2 * wide_cos.shape[0] * spectra[0].shape[0]
    summed = jnp.einsum("rkf,nk->rnf", arrived_real, wide_cos, precision=PRECISE) - jnp.einsum(
        "rkf,nk->rnf", arrived_imag, wide_sin, precision=PRECISE
    )
    return summed * (1.0 / padded_len)


def spectrum(block_data, tables):
    return forward_columns(spread_out(block_data[:, None, :]), tables)


def signal_rows(spectra, tables):
    arrived = bring_back(inverse_columns(spectra, tables))
    return arrived.reshape(arrived.shape[0], -1)


def take_range(spectra, start, stop):
    return (spectra[0][..., start:stop], spectra[1][..., start:stop])


def joined(first_pair, second_pair):
    return (
        jnp.concatenate([first_pair[0], second_pair[0]], axis=-1),
        jnp.concatenate([first_pair[1], second_pair[1]], axis=-1),
    )


def filtered(spectra, filters, conjugate):
    groups = filters[0].shape[-1]
    shape_in = spectra[0].shape
    split_shape = shape_in[:-1] + (groups, shape_in[-1] // groups)
    left_real = spectra[0].reshape(split_shape)
    left_imag = spectra[1].reshape(split_shape)
    right_real = filters[0][..., None]
    right_imag = filters[1][..., None] * (-1.0 if conjugate else 1.0)
    out_real = left_real * right_real - left_imag * right_imag
    out_imag = left_real * right_imag + left_imag * right_real
    return (out_real.reshape(shape_in), out_imag.reshape(shape_in))


def pooled(first_pair, second_pair, groups):
    shape_in = first_pair[0].shape
    split_shape = shape_in[:-1] + (groups, shape_in[-1] // groups)
    left_real = first_pair[0].reshape(split_shape)
    left_imag = first_pair[1].reshape(split_shape)
    right_real = second_pair[0].reshape(split_shape)
    right_imag = second_pair[1].reshape(split_shape)
    out_real = jnp.sum(left_real * right_real + left_imag * right_imag, axis=-1)
    out_imag = jnp.sum(left_real * right_imag - left_imag * right_real, axis=-1)
    return (out_real, out_imag)


def project(pooled_in, target, weights, w_cols):
    gathered = lax.all_gather(pooled_in, "chan", axis=1, tiled=True)
    output = jnp.dot(gathered, w_cols, preferred_element_type=jnp.float32)
    deviation = (weights[:, None] * (output - target.astype(jnp.float32))).astype(jnp.bfloat16)
    partial_w = lax.dot_general(
        gathered, deviation, (((0,), (0,)), ((), ())), preferred_element_type=jnp.float32
    )
    weight_grad = lax.psum_scatter(partial_w, "seq", scatter_dimension=0, tiled=True)
    channel_back = lax.psum_scatter(
        lax.dot_general(
            w_cols, deviation, (((1,), (1,)), ((), ())), preferred_element_type=jnp.float32
        ),
        "chan",
        scatter_dimension=0,
        tiled=True,
    )
    back_outer = channel_back.T
    return (back_outer, weight_grad)


def per_device(
    values,
    gate_inner,
    gate_outer,
    filter_one,
    filter_two,
    teacher,
    w_out,
    gene_ids,
    cell_lengths,
    gene_weights,
):
    shard_count = lax.axis_size("seq")
    position = lax.axis_index("seq")
    length = values.shape[0]
    channels = values.shape[1]
    groups = filter_one.shape[0]
    tables = make_tables(length, shard_count, position)
    token_pos = position * length + jnp.arange(length, dtype=jnp.int32)
    starts = jnp.cumsum(cell_lengths) - cell_lengths
    opening = jnp.any(token_pos[:, None] == starts[None, :], axis=1)
    weights = jnp.take(gene_weights, gene_ids, axis=0) * jnp.where(opening, 0.0, 1.0)
    stacked = jnp.concatenate([values.astype(jnp.float32), filter_one.T, filter_two.T], axis=1)
    spectra = spectrum(stacked, tables)
    spec_values = take_range(spectra, 0, channels)
    spec_one = take_range(spectra, channels, channels + groups)
    spec_two = take_range(spectra, channels + groups, channels + 2 * groups)
    first_conv = signal_rows(filtered(spec_values, spec_one, False), tables)
    spec_inner = spectrum(gate_inner * first_conv, tables)
    second_conv = signal_rows(filtered(spec_inner, spec_two, False), tables)
    pooled_in = (gate_outer * second_conv).astype(jnp.bfloat16)
    back_outer, grad_w_out = project(pooled_in, teacher, weights, w_out)
    grad_outer = (back_outer * second_conv).astype(jnp.bfloat16)
    spec_second = spectrum(back_outer * gate_outer, tables)
    merged = signal_rows(
        joined(filtered(spec_second, spec_two, True), pooled(spec_inner, spec_second, groups)),
        tables,
    )
    back_inner = merged[:, :channels]
    grad_two = merged[:, channels:]
    grad_inner = (back_inner * first_conv).astype(jnp.bfloat16)
    spec_first = spectrum(back_inner * gate_inner, tables)
    merged = signal_rows(
        joined(filtered(spec_first, spec_one, True), pooled(spec_values, spec_first, groups)),
        tables,
    )
    grad_values = merged[:, :channels].astype(jnp.bfloat16)
    grad_one = merged[:, channels:]
    return (grad_values, grad_inner, grad_outer, grad_one.T, grad_two.T, grad_w_out)


def solution(mesh):
    return jax.shard_map(
        per_device,
        mesh=mesh,
        in_specs=(
            P("seq", "chan"),
            P("seq", "chan"),
            P("seq", "chan"),
            P("chan", "seq"),
            P("chan", "seq"),
            P("seq", "chan"),
            P(None, "chan"),
            P("seq"),
            P(),
            P(),
        ),
        out_specs=(
            P("seq", "chan"),
            P("seq", "chan"),
            P("seq", "chan"),
            P("chan", "seq"),
            P("chan", "seq"),
            P("seq", "chan"),
        ),
        check_vma=False,
    )
```

profile of v0, /device:TPU:4, one launch (start us, length us, event | category | flops | bytes accessed | tf_op | source)
XLA Modules:
  0.0 558.9 jit_solution(16846920802349217116)
XLA Ops:
  8.0 0.8 convert_element_type.117
  8.8 0.7 copy-done.5
  9.5 0.7 copy.332
  10.2 16.0 %all-to-all-start = ((f32[128,1,66]{2,1,0:T(1,128)}), f32[128,1,66]{2,1,0:T(1,128)S(1)}, u32[]{:S(2)}, u32[]{:S(2)}) async-start(f32[128,1,66]{2,1,0:T(1,128)} %copy.332), calls=%async_computation | async-start | bytes 131072 | tf_op jit(solution)/shard_map/all_to_all | solution.py:33
  26.3 12.4 %all-to-all-done = f32[128,1,66]{2,1,0:T(1,128)S(1)} async-done(((f32[128,1,66]{2,1,0:T(1,128)}), f32[128,1,66]{2,1,0:T(1,128)S(1)}, u32[]{:S(2)}, u32[]{:S(2)}) %all-to-all-start) | async-done | bytes 33824 | tf_op jit(solution)/shard_map/all_to_all | solution.py:33
  39.6 0.9 copy.334
  40.5 3.9 all-to-all-start.1
  44.5 14.4 %all-to-all-done.1 = f32[4,64,132]{2,0,1:T(4,128)S(1)} async-done(((f32[4,64,132]{2,0,1:T(4,128)}), f32[4,64,132]{2,0,1:T(4,128)S(1)}, u32[]{:S(2)}, u32[]{:S(2)}) %all-to-all-start.1) | async-done | bytes 135200 | tf_op jit(solution)/shard_map/all_to_all | solution.py:37
  59.5 0.6 fusion.30
  60.1 0.6 fusion.31
  62.3 18.0 %all_to_all.276 = f32[128,2,128]{2,1,0:T(2,128)S(1)} all-to-all(f32[128,2,128]{2,1,0:T(2,128)S(1)} %copy.341), channel_id=1, replica_groups=mesh['seq'=32,'chan'=16] {'seq'}, dimensions={0} | all-to-all | bytes 262144 | tf_op jit(solution)/shard_map/all_to_all | solution.py:33
  81.1 0.7 reshape.508
  81.8 3.9 all-to-all-start.3
  85.9 12.3 %all-to-all-done.3 = f32[32,1,256]{2,1,0:T(1,128)S(1)} async-done(((f32[32,1,256]{2,1,0:T(1,128)}), f32[32,1,256]{2,1,0:T(1,128)S(1)}, u32[]{:S(2)}, u32[]{:S(2)}) %all-to-all-start.3) | async-done | bytes 32800 | tf_op jit(solution)/shard_map/all_to_all | solution.py:37
  98.7 0.7 reduce.12
  99.6 0.8 reduce.13
  100.5 15.4 %all_to_all.277 = f32[32,1,256]{2,1,0:T(1,128)S(1)} all-to-all(f32[32,1,256]{2,1,0:T(1,128)S(1)} %reshape.510), channel_id=1, replica_groups=mesh['seq'=32,'chan'=16] {'seq'}, dimensions={0} | all-to-all | bytes 65536 | tf_op jit(solution)/shard_map/all_to_all | solution.py:33
  115.8 0.7 reduce.14
  117.6 0.7 copy.347
  118.3 4.0 all-to-all-start.5
  122.4 0.6 copy-done.8
  123.4 12.1 %all-to-all-done.5 = f32[4,64,128]{2,0,1:T(4,128)S(1)} async-done(((f32[4,64,128]{2,0,1:T(4,128)}), f32[4,64,128]{2,0,1:T(4,128)S(1)}, u32[]{:S(2)}, u32[]{:S(2)}) %all-to-all-start.5) | async-done | bytes 131104 | tf_op jit(solution)/shard_map/all_to_all | solution.py:37
  138.2 0.7 copy.357
  139.0 4.2 all-to-all-start.6
  143.2 1.1 gather_fusion
  144.4 11.6 %all-to-all-done.6 = f32[128,2,128]{2,1,0:T(2,128)S(1)} async-done(((f32[128,2,128]{2,1,0:T(2,128)}), f32[128,2,128]{2,1,0:T(2,128)S(1)}, u32[]{:S(2)}, u32[]{:S(2)}) %all-to-all-start.6) | async-done | bytes 131104 | tf_op jit(solution)/shard_map/all_to_all | solution.py:33
  156.8 0.7 reshape.512
  157.5 3.9 all-to-all-start.7
  161.7 12.2 %all-to-all-done.7 = f32[32,1,256]{2,1,0:T(1,128)S(1)} async-done(((f32[32,1,256]{2,1,0:T(1,128)}), f32[32,1,256]{2,1,0:T(1,128)S(1)}, u32[]{:S(2)}, u32[]{:S(2)}) %all-to-all-start.7) | async-done | bytes 32800 | tf_op jit(solution)/shard_map/all_to_all | solution.py:37
  173.8 0.7 reduce.15
  174.8 36.0 %all_gather.3 = bf16[128,1024]{0,1:T(8,128)(2,1)S(1)} all-gather(bf16[128,64]{0,1:T(8,128)(2,1)S(1)} %copy.361), channel_id=1, replica_groups=mesh['seq'=32,'chan'=16] {'chan'}, dimensions={1}, use_global_device_ids=true | all-gather | bytes 278528 | tf_op jit(solution)/shard_map/all_gather | solution.py:142
  211.2 1.0 copy.391
  212.2 71.3 %reduce-scatter.7.cloned.1.call-done = f32[64,128]{1,0:T(8,128)} async-done(((f32[1024,128]{1,0:T(8,128)}), f32[64,128]{1,0:T(8,128)}) %reduce-scatter.7.cloned.1.call-update) | async-done | bytes 32784
  283.5 0.8 copy.392
  284.4 0.8 reduce.16
  285.3 22.2 %all_to_all.278 = f32[32,1,256]{2,1,0:T(1,128)S(1)} all-to-all(f32[32,1,256]{2,1,0:T(1,128)S(1)} %reshape.514), channel_id=1, replica_groups=mesh['seq'=32,'chan'=16] {'seq'}, dimensions={0} | all-to-all | bytes 65536 | tf_op jit(solution)/shard_map/all_to_all | solution.py:33
  307.5 0.7 reduce.17
  309.3 0.7 copy.364
  310.0 3.9 all-to-all-start.9
  313.9 13.1 %all-to-all-done.9 = f32[4,64,128]{2,0,1:T(4,128)S(1)} async-done(((f32[4,64,128]{2,0,1:T(4,128)}), f32[4,64,128]{2,0,1:T(4,128)S(1)}, u32[]{:S(2)}, u32[]{:S(2)}) %all-to-all-start.9) | async-done | bytes 131104 | tf_op jit(solution)/shard_map/all_to_all | solution.py:37
  329.0 0.6 fusion.28
  329.6 0.6 fusion.29
  330.5 17.8 %all_to_all.279 = f32[128,2,130]{2,1,0:T(2,128)S(1)} all-to-all(f32[128,2,130]{2,1,0:T(2,128)S(1)} %copy.374), channel_id=1, replica_groups=mesh['seq'=32,'chan'=16] {'seq'}, dimensions={0} | all-to-all | bytes 266240 | tf_op jit(solution)/shard_map/all_to_all | solution.py:33
  349.3 17.2 %all_to_all.280 = f32[4,32,65]{2,0,1:T(4,128)S(1)} all-to-all(f32[4,32,65]{2,0,1:T(4,128)S(1)} %copy.376), channel_id=1, replica_groups=mesh['seq'=32,'chan'=16] {'seq'}, dimensions={1} | all-to-all | bytes 66560 | tf_op jit(solution)/shard_map/all_to_all | solution.py:37
  366.5 0.8 reduce.18
  367.4 15.3 %all_to_all.281 = f32[32,1,256]{2,1,0:T(1,128)S(1)} all-to-all(f32[32,1,256]{2,1,0:T(1,128)S(1)} %reshape.516), channel_id=1, replica_groups=mesh['seq'=32,'chan'=16] {'seq'}, dimensions={0} | all-to-all | bytes 65536 | tf_op jit(solution)/shard_map/all_to_all | solution.py:33
  382.7 0.7 reduce.19
  384.5 0.7 copy.379
  385.2 4.1 all-to-all-start.13
  389.3 12.9 %all-to-all-done.13 = f32[4,64,128]{2,0,1:T(4,128)S(1)} async-done(((f32[4,64,128]{2,0,1:T(4,128)}), f32[4,64,128]{2,0,1:T(4,128)S(1)}, u32[]{:S(2)}, u32[]{:S(2)}) %all-to-all-start.13) | async-done | bytes 131104 | tf_op jit(solution)/shard_map/all_to_all | solution.py:37
  404.5 0.6 fusion.27
  405.3 0.8 copy.385
  406.1 3.9 all-to-all-start.14
  410.0 1.0 fusion.357
  411.1 0.7 copy.390
  411.8 0.7 copy.389
  412.5 12.1 %all-to-all-done.14 = f32[128,2,130]{2,1,0:T(2,128)S(1)} async-done(((f32[128,2,130]{2,1,0:T(2,128)}), f32[128,2,130]{2,1,0:T(2,128)S(1)}, u32[]{:S(2)}, u32[]{:S(2)}) %all-to-all-start.14) | async-done | bytes 133152 | tf_op jit(solution)/shard_map/all_to_all | solution.py:33
  425.4 0.7 copy.387
  426.0 5.0 all-to-all-start.15
  431.0 0.7 slice_reduce_fusion
  431.7 11.8 %all-to-all-done.15 = f32[4,32,65]{2,0,1:T(4,128)S(1)} async-done(((f32[4,32,65]{2,0,1:T(4,128)}), f32[4,32,65]{2,0,1:T(4,128)S(1)}, u32[]{:S(2)}, u32[]{:S(2)}) %all-to-all-start.15) | async-done | bytes 33312 | tf_op jit(solution)/shard_map/all_to_all | solution.py:37
  443.5 0.7 copy.388
  444.2 0.7 slice_reduce_fusion.1
  444.9 106.5 %reduce-scatter.5.cloned.1.call-done = f32[32,64]{1,0:T(8,128)} async-done(((f32[1024,64]{1,0:T(8,128)}), f32[32,64]{1,0:T(8,128)}) %reduce-scatter.5.cloned.1.call-update) | async-done | bytes 8208 | tf_op jit(solution)/shard_map/reduce_scatter | solution.py:148
  (168 shorter events, 18.8 us)
Async XLA Ops:
  8.0 202.8 %copy-start = (bf16[1024,64]{0,1:T(8,128)(2,1)S(1)}, bf16[1024,64]{0,1:T(8,128)(2,1)}, u32[]{:S(2)}) copy-start(bf16[1024,64]{0,1:T(8,128)(2,1)} %param.16) | copy-start | bytes 393220
  8.8 0.7 copy-start.5
  8.8 0.7 copy-start.6
  10.2 28.5 %all-to-all-start = ((f32[128,1,66]{2,1,0:T(1,128)}), f32[128,1,66]{2,1,0:T(1,128)S(1)}, u32[]{:S(2)}, u32[]{:S(2)}) async-start(f32[128,1,66]{2,1,0:T(1,128)} %copy.332), calls=%async_computation | async-start | bytes 131072 | tf_op jit(solution)/shard_map/all_to_all | solution.py:33
  40.5 18.4 %all-to-all-start.1 = ((f32[4,64,132]{2,0,1:T(4,128)}), f32[4,64,132]{2,0,1:T(4,128)S(1)}, u32[]{:S(2)}, u32[]{:S(2)}) async-start(f32[4,64,132]{2,0,1:T(4,128)} %copy.334), calls=%async_computation.1 | async-start | bytes 524288 | tf_op jit(solution)/shard_map/all_to_all | solution.py:37
  81.8 4.0 copy-start.2
  81.8 16.4 %all-to-all-start.3 = ((f32[32,1,256]{2,1,0:T(1,128)}), f32[32,1,256]{2,1,0:T(1,128)S(1)}, u32[]{:S(2)}, u32[]{:S(2)}) async-start(f32[32,1,256]{2,1,0:T(1,128)} %reshape.508), calls=%async_computation.3 | async-start | bytes 65536 | tf_op jit(solution)/shard_map/all_to_all | solution.py:37
  118.3 4.0 copy-start.7
  118.3 17.1 %all-to-all-start.5 = ((f32[4,64,128]{2,0,1:T(4,128)}), f32[4,64,128]{2,0,1:T(4,128)S(1)}, u32[]{:S(2)}, u32[]{:S(2)}) async-start(f32[4,64,128]{2,0,1:T(4,128)} %copy.347), calls=%async_computation.5 | async-start | bytes 262144 | tf_op jit(solution)/shard_map/all_to_all | solution.py:37
  122.3 0.7 copy-start.8
  139.0 4.2 copy-start.1
  139.0 17.1 %all-to-all-start.6 = ((f32[128,2,128]{2,1,0:T(2,128)}), f32[128,2,128]{2,1,0:T(2,128)S(1)}, u32[]{:S(2)}, u32[]{:S(2)}) async-start(f32[128,2,128]{2,1,0:T(2,128)} %copy.357), calls=%async_computation.6 | async-start | bytes 262144 | tf_op jit(solution)/shard_map/all_to_all | solution.py:33
  157.5 4.0 copy-start.3
  157.5 16.3 %all-to-all-start.7 = ((f32[32,1,256]{2,1,0:T(1,128)}), f32[32,1,256]{2,1,0:T(1,128)S(1)}, u32[]{:S(2)}, u32[]{:S(2)}) async-start(f32[32,1,256]{2,1,0:T(1,128)} %reshape.512), calls=%async_computation.7 | async-start | bytes 65536 | tf_op jit(solution)/shard_map/all_to_all | solution.py:37
  161.5 122.1 %reduce-scatter.7.cloned.1.call-start = ((), (), s32[]{:S(2)}) async-start(), calls=%async_computation.19 | async-start | bytes 557056
  174.8 36.0 %copy-start.4 = (bf16[128,64]{0,1:T(8,128)(2,1)S(1)}, bf16[128,64]{0,1:T(8,128)(2,1)}, u32[]{:S(2)}) copy-start(bf16[128,64]{0,1:T(8,128)(2,1)} %param.15) | copy-start | bytes 49156
  310.0 17.0 %all-to-all-start.9 = ((f32[4,64,128]{2,0,1:T(4,128)}), f32[4,64,128]{2,0,1:T(4,128)S(1)}, u32[]{:S(2)}, u32[]{:S(2)}) async-start(f32[4,64,128]{2,0,1:T(4,128)} %copy.364), calls=%async_computation.9 | async-start | bytes 262144 | tf_op jit(solution)/shard_map/all_to_all | solution.py:37
  385.2 17.0 %all-to-all-start.13 = ((f32[4,64,128]{2,0,1:T(4,128)}), f32[4,64,128]{2,0,1:T(4,128)S(1)}, u32[]{:S(2)}, u32[]{:S(2)}) async-start(f32[4,64,128]{2,0,1:T(4,128)} %copy.379), calls=%async_computation.13 | async-start | bytes 262144 | tf_op jit(solution)/shard_map/all_to_all | solution.py:37
  406.1 18.4 %all-to-all-start.14 = ((f32[128,2,130]{2,1,0:T(2,128)}), f32[128,2,130]{2,1,0:T(2,128)S(1)}, u32[]{:S(2)}, u32[]{:S(2)}) async-start(f32[128,2,130]{2,1,0:T(2,128)} %copy.385), calls=%async_computation.14 | async-start | bytes 524288 | tf_op jit(solution)/shard_map/all_to_all | solution.py:33
  410.0 141.4 %reduce-scatter.5.cloned.1.call-start = ((), (), s32[]{:S(2)}) async-start(), calls=%async_computation.18 | async-start | bytes 540672 | tf_op jit(solution)/shard_map/reduce_scatter | solution.py:148
  426.0 17.5 %all-to-all-start.15 = ((f32[4,32,65]{2,0,1:T(4,128)}), f32[4,32,65]{2,0,1:T(4,128)S(1)}, u32[]{:S(2)}, u32[]{:S(2)}) async-start(f32[4,32,65]{2,0,1:T(4,128)} %copy.387), calls=%async_computation.15 | async-start | bytes 131072 | tf_op jit(solution)/shard_map/all_to_all | solution.py:37
Sparse Core Ops, SparseCore 0:
  212.4 71.1 reduce-scatter.6
Sparse Core Ops, SparseCore 1:
  416.3 135.0 reduce-scatter.4
where the time goes:
time: 560 us; the launch traced here: 559 us
  waiting for transfers between devices  303 us (54%)
  blocking collectives  142 us (25%)
  starting transfers between devices  52.7 us (9%)
  local copies, waits for them, and re-layouts  20.5 us (4%)
  between operations  16.6 us (3%)
  matrix products  16 us (3%)
  other arithmetic  8.36 us (1%)
    reduce_scatter x1, waiting for transfers between devices, project(): lax.psum_scatter(partial_w, 'seq', scatter_dimension=0, tiled=True)  107 us
    all_to_all x7, waiting for transfers between devices, bring_back(): lax.all_to_all(packed, 'seq', split_axis=1, concat_axis=0, tiled=True)  88.8 us
    all_to_all x5, blocking collectives, spread_out(): lax.all_to_all(packed, 'seq', split_axis=0, concat_axis=1, tiled=True)  88.7 us
    unnamed x3, waiting for transfers between devices  71.3 us
    all_to_all x3, waiting for transfers between devices, spread_out(): lax.all_to_all(packed, 'seq', split_axis=0, concat_axis=1, tiled=True)  36 us
    all_gather x1, blocking collectives, project(): gathered = lax.all_gather(pooled_in, 'chan', axis=1, tiled=True)  36 us
    all_to_all x7, starting transfers between devices, bring_back(): lax.all_to_all(packed, 'seq', split_axis=1, concat_axis=0, tiled=True)  28.6 us
    all_to_all x3, starting transfers between devices, spread_out(): lax.all_to_all(packed, 'seq', split_axis=0, concat_axis=1, tiled=True)  24 us
  transfers between devices with their start and end apart: 12, of which 12 were waited for; matrix products, arithmetic and copies ran while one was open for 1% of the time, Pallas kernels for 0%

commit v1 on v0

--- a/solution.py
+++ b/solution.py
@@ -139,7 +139,9 @@
 
 
 def project(pooled_in, target, weights, w_cols):
-    gathered = lax.all_gather(pooled_in, "chan", axis=1, tiled=True)
+    gathered = jnp.concatenate(
+        lax.all_to_all(jnp.stack([pooled_in] * lax.axis_size("chan")), "chan", 0, 0), axis=1
+    )
     output = jnp.dot(gathered, w_cols, preferred_element_type=jnp.float32)
     deviation = (weights[:, None] * (output - target.astype(jnp.float32))).astype(jnp.bfloat16)
     partial_w = lax.dot_general(

time: 560 us -> 539 us (0.963)
  the two profiles are of different devices: /device:TPU:4 before, /device:TPU:2 now
where the time goes in v1:
time: 539 us; the launch traced here: 537 us
  waiting for transfers between devices  308 us (57%)
  blocking collectives  106 us (20%)
  starting transfers between devices  60.6 us (11%)
  local copies, waits for them, and re-layouts  21.3 us (4%)
  between operations  16.6 us (3%)
  matrix products  16.1 us (3%)
  other arithmetic  8.36 us (2%)
    reduce_scatter x1, waiting for transfers between devices, project(): lax.psum_scatter(partial_w, 'seq', scatter_dimension=0, tiled=True)  103 us
    all_to_all x7, waiting for transfers between devices, bring_back(): lax.all_to_all(packed, 'seq', split_axis=1, concat_axis=0, tiled=True)  89.5 us
    all_to_all x5, blocking collectives, spread_out(): lax.all_to_all(packed, 'seq', split_axis=0, concat_axis=1, tiled=True)  88.6 us
    unnamed x3, waiting for transfers between devices  72.7 us
    all_to_all x3, waiting for transfers between devices, spread_out(): lax.all_to_all(packed, 'seq', split_axis=0, concat_axis=1, tiled=True)  36.4 us
    all_to_all x7, starting transfers between devices, bring_back(): lax.all_to_all(packed, 'seq', split_axis=1, concat_axis=0, tiled=True)  28.6 us
    all_to_all x3, starting transfers between devices, spread_out(): lax.all_to_all(packed, 'seq', split_axis=0, concat_axis=1, tiled=True)  23.9 us
    all_to_all x1, blocking collectives, bring_back(): lax.all_to_all(packed, 'seq', split_axis=1, concat_axis=0, tiled=True)  17.5 us
  transfers between devices with their start and end apart: 13, of which 13 were waited for; matrix products, arithmetic and copies ran while one was open for 1% of the time, Pallas kernels for 0%

profile of v1, /device:TPU:2, one launch (start us, length us, event | category | flops | bytes accessed | tf_op | source)
XLA Modules:
  0.0 537.4 jit_solution(7701910242564440795)
XLA Ops:
  8.0 0.8 convert_element_type.117
  8.8 0.7 copy-done.5
  9.5 0.7 copy.334
  10.2 16.0 %all-to-all-start = ((f32[128,1,66]{2,1,0:T(1,128)}), f32[128,1,66]{2,1,0:T(1,128)S(1)}, u32[]{:S(2)}, u32[]{:S(2)}) async-start(f32[128,1,66]{2,1,0:T(1,128)} %copy.334), calls=%async_computation | async-start | bytes 131072 | tf_op jit(solution)/shard_map/all_to_all | solution.py:33
  26.3 12.4 %all-to-all-done = f32[128,1,66]{2,1,0:T(1,128)S(1)} async-done(((f32[128,1,66]{2,1,0:T(1,128)}), f32[128,1,66]{2,1,0:T(1,128)S(1)}, u32[]{:S(2)}, u32[]{:S(2)}) %all-to-all-start) | async-done | bytes 33824 | tf_op jit(solution)/shard_map/all_to_all | solution.py:33
  39.6 0.9 copy.336
  40.5 3.9 all-to-all-start.1
  44.5 14.4 %all-to-all-done.1 = f32[4,64,132]{2,0,1:T(4,128)S(1)} async-done(((f32[4,64,132]{2,0,1:T(4,128)}), f32[4,64,132]{2,0,1:T(4,128)S(1)}, u32[]{:S(2)}, u32[]{:S(2)}) %all-to-all-start.1) | async-done | bytes 135200 | tf_op jit(solution)/shard_map/all_to_all | solution.py:37
  59.5 0.6 fusion.30
  60.1 0.6 fusion.31
  62.3 18.0 %all_to_all.281 = f32[128,2,128]{2,1,0:T(2,128)S(1)} all-to-all(f32[128,2,128]{2,1,0:T(2,128)S(1)} %copy.343), channel_id=1, replica_groups=mesh['seq'=32,'chan'=16] {'seq'}, dimensions={0} | all-to-all | bytes 262144 | tf_op jit(solution)/shard_map/all_to_all | solution.py:33
  81.1 0.7 reshape.518
  81.8 3.9 all-to-all-start.3
  85.9 12.3 %all-to-all-done.3 = f32[32,1,256]{2,1,0:T(1,128)S(1)} async-done(((f32[32,1,256]{2,1,0:T(1,128)}), f32[32,1,256]{2,1,0:T(1,128)S(1)}, u32[]{:S(2)}, u32[]{:S(2)}) %all-to-all-start.3) | async-done | bytes 32800 | tf_op jit(solution)/shard_map/all_to_all | solution.py:37
  98.7 0.7 reduce.12
  99.5 0.8 reduce.13
  100.4 15.4 %all_to_all.282 = f32[32,1,256]{2,1,0:T(1,128)S(1)} all-to-all(f32[32,1,256]{2,1,0:T(1,128)S(1)} %reshape.520), channel_id=1, replica_groups=mesh['seq'=32,'chan'=16] {'seq'}, dimensions={0} | all-to-all | bytes 65536 | tf_op jit(solution)/shard_map/all_to_all | solution.py:33
  115.8 0.7 reduce.14
  117.6 0.7 copy.349
  118.3 3.8 all-to-all-start.5
  122.4 12.9 %all-to-all-done.5 = f32[4,64,128]{2,0,1:T(4,128)S(1)} async-done(((f32[4,64,128]{2,0,1:T(4,128)}), f32[4,64,128]{2,0,1:T(4,128)S(1)}, u32[]{:S(2)}, u32[]{:S(2)}) %all-to-all-start.5) | async-done | bytes 131104 | tf_op jit(solution)/shard_map/all_to_all | solution.py:37
  138.0 0.8 copy.359
  138.8 4.0 all-to-all-start.6
  142.8 0.6 copy-done.8
  143.7 12.0 %all-to-all-done.6 = f32[128,2,128]{2,1,0:T(2,128)S(1)} async-done(((f32[128,2,128]{2,1,0:T(2,128)}), f32[128,2,128]{2,1,0:T(2,128)S(1)}, u32[]{:S(2)}, u32[]{:S(2)}) %all-to-all-start.6) | async-done | bytes 131104 | tf_op jit(solution)/shard_map/all_to_all | solution.py:33
  156.5 0.7 reshape.522
  157.2 3.9 all-to-all-start.7
  161.3 12.2 %all-to-all-done.7 = f32[32,1,256]{2,1,0:T(1,128)S(1)} async-done(((f32[32,1,256]{2,1,0:T(1,128)}), f32[32,1,256]{2,1,0:T(1,128)S(1)}, u32[]{:S(2)}, u32[]{:S(2)}) %all-to-all-start.7) | async-done | bytes 32800 | tf_op jit(solution)/shard_map/all_to_all | solution.py:37
  173.5 0.7 reduce.15
  174.4 0.8 stack.2
  175.2 8.1 %all-to-all-start.8 = ((bf16[16,128,64]{1,2,0:T(8,128)(2,1)}), bf16[16,128,64]{1,2,0:T(8,128)(2,1)S(1)}, u32[]{:S(2)}, u32[]{:S(2)}) async-start(bf16[16,128,64]{1,2,0:T(8,128)(2,1)} %stack.2), calls=%async_computation.8 | async-start | bytes 524288 | tf_op jit(solution)/shard_map/all_to_all | solution.py:143
  183.4 1.1 gather_fusion
  184.7 6.8 %all-to-all-done.8 = bf16[16,128,64]{1,2,0:T(8,128)(2,1)S(1)} async-done(((bf16[16,128,64]{1,2,0:T(8,128)(2,1)}), bf16[16,128,64]{1,2,0:T(8,128)(2,1)S(1)}, u32[]{:S(2)}, u32[]{:S(2)}) %all-to-all-start.8) | async-done | bytes 262176 | tf_op jit(solution)/shard_map/all_to_all | solution.py:143
  192.0 1.0 copy.393
  193.0 72.6 %reduce-scatter.7.cloned.1.call-done = f32[64,128]{1,0:T(8,128)} async-done(((f32[1024,128]{1,0:T(8,128)}), f32[64,128]{1,0:T(8,128)}) %reduce-scatter.7.cloned.1.call-update) | async-done | bytes 32784
  265.6 0.8 copy.394
  266.5 0.8 reduce.16
  267.4 22.2 %all_to_all.283 = f32[32,1,256]{2,1,0:T(1,128)S(1)} all-to-all(f32[32,1,256]{2,1,0:T(1,128)S(1)} %reshape.524), channel_id=1, replica_groups=mesh['seq'=32,'chan'=16] {'seq'}, dimensions={0} | all-to-all | bytes 65536 | tf_op jit(solution)/shard_map/all_to_all | solution.py:33
  289.6 0.7 reduce.17
  291.3 0.7 copy.366
  292.1 3.8 all-to-all-start.10
  295.9 13.0 %all-to-all-done.10 = f32[4,64,128]{2,0,1:T(4,128)S(1)} async-done(((f32[4,64,128]{2,0,1:T(4,128)}), f32[4,64,128]{2,0,1:T(4,128)S(1)}, u32[]{:S(2)}, u32[]{:S(2)}) %all-to-all-start.10) | async-done | bytes 131104 | tf_op jit(solution)/shard_map/all_to_all | solution.py:37
  310.9 0.6 fusion.28
  312.5 17.8 %all_to_all.284 = f32[128,2,130]{2,1,0:T(2,128)S(1)} all-to-all(f32[128,2,130]{2,1,0:T(2,128)S(1)} %copy.376), channel_id=1, replica_groups=mesh['seq'=32,'chan'=16] {'seq'}, dimensions={0} | all-to-all | bytes 266240 | tf_op jit(solution)/shard_map/all_to_all | solution.py:33
  331.2 17.5 %all_to_all.285 = f32[4,32,65]{2,0,1:T(4,128)S(1)} all-to-all(f32[4,32,65]{2,0,1:T(4,128)S(1)} %copy.378), channel_id=1, replica_groups=mesh['seq'=32,'chan'=16] {'seq'}, dimensions={1} | all-to-all | bytes 66560 | tf_op jit(solution)/shard_map/all_to_all | solution.py:37
  348.7 0.8 reduce.18
  349.6 15.3 %all_to_all.286 = f32[32,1,256]{2,1,0:T(1,128)S(1)} all-to-all(f32[32,1,256]{2,1,0:T(1,128)S(1)} %reshape.526), channel_id=1, replica_groups=mesh['seq'=32,'chan'=16] {'seq'}, dimensions={0} | all-to-all | bytes 65536 | tf_op jit(solution)/shard_map/all_to_all | solution.py:33
  364.9 0.7 reduce.19
  366.7 0.7 copy.381
  367.4 4.1 all-to-all-start.14
  371.5 12.8 %all-to-all-done.14 = f32[4,64,128]{2,0,1:T(4,128)S(1)} async-done(((f32[4,64,128]{2,0,1:T(4,128)}), f32[4,64,128]{2,0,1:T(4,128)S(1)}, u32[]{:S(2)}, u32[]{:S(2)}) %all-to-all-start.14) | async-done | bytes 131104 | tf_op jit(solution)/shard_map/all_to_all | solution.py:37
  387.4 0.8 copy.387
  388.2 3.9 all-to-all-start.15
  392.1 1.0 fusion.357
  393.2 0.7 copy.392
  393.9 0.7 copy.391
  394.6 11.9 %all-to-all-done.15 = f32[128,2,130]{2,1,0:T(2,128)S(1)} async-done(((f32[128,2,130]{2,1,0:T(2,128)}), f32[128,2,130]{2,1,0:T(2,128)S(1)}, u32[]{:S(2)}, u32[]{:S(2)}) %all-to-all-start.15) | async-done | bytes 133152 | tf_op jit(solution)/shard_map/all_to_all | solution.py:33
  407.4 0.7 copy.389
  408.0 5.1 all-to-all-start.16
  413.1 0.7 slice_reduce_fusion
  413.8 11.8 %all-to-all-done.16 = f32[4,32,65]{2,0,1:T(4,128)S(1)} async-done(((f32[4,32,65]{2,0,1:T(4,128)}), f32[4,32,65]{2,0,1:T(4,128)S(1)}, u32[]{:S(2)}, u32[]{:S(2)}) %all-to-all-start.16) | async-done | bytes 33312 | tf_op jit(solution)/shard_map/all_to_all | solution.py:37
  425.6 0.7 copy.390
  426.3 0.7 slice_reduce_fusion.1
  427.0 102.9 %reduce-scatter.5.cloned.1.call-done = f32[32,64]{1,0:T(8,128)} async-done(((f32[1024,64]{1,0:T(8,128)}), f32[32,64]{1,0:T(8,128)}) %reduce-scatter.5.cloned.1.call-update) | async-done | bytes 8208 | tf_op jit(solution)/shard_map/reduce_scatter | solution.py:150
  (170 shorter events, 20.1 us)
Async XLA Ops:
  8.0 183.5 %copy-start = (bf16[1024,64]{0,1:T(8,128)(2,1)S(1)}, bf16[1024,64]{0,1:T(8,128)(2,1)}, u32[]{:S(2)}) copy-start(bf16[1024,64]{0,1:T(8,128)(2,1)} %param.16) | copy-start | bytes 393220
  8.8 0.7 copy-start.5
  8.8 0.7 copy-start.6
  10.2 28.5 %all-to-all-start = ((f32[128,1,66]{2,1,0:T(1,128)}), f32[128,1,66]{2,1,0:T(1,128)S(1)}, u32[]{:S(2)}, u32[]{:S(2)}) async-start(f32[128,1,66]{2,1,0:T(1,128)} %copy.334), calls=%async_computation | async-start | bytes 131072 | tf_op jit(solution)/shard_map/all_to_all | solution.py:33
  40.5 18.4 %all-to-all-start.1 = ((f32[4,64,132]{2,0,1:T(4,128)}), f32[4,64,132]{2,0,1:T(4,128)S(1)}, u32[]{:S(2)}, u32[]{:S(2)}) async-start(f32[4,64,132]{2,0,1:T(4,128)} %copy.336), calls=%async_computation.1 | async-start | bytes 524288 | tf_op jit(solution)/shard_map/all_to_all | solution.py:37
  81.8 3.9 copy-start.2
  81.8 16.4 %all-to-all-start.3 = ((f32[32,1,256]{2,1,0:T(1,128)}), f32[32,1,256]{2,1,0:T(1,128)S(1)}, u32[]{:S(2)}, u32[]{:S(2)}) async-start(f32[32,1,256]{2,1,0:T(1,128)} %reshape.518), calls=%async_computation.3 | async-start | bytes 65536 | tf_op jit(solution)/shard_map/all_to_all | solution.py:37
  118.3 17.0 %all-to-all-start.5 = ((f32[4,64,128]{2,0,1:T(4,128)}), f32[4,64,128]{2,0,1:T(4,128)S(1)}, u32[]{:S(2)}, u32[]{:S(2)}) async-start(f32[4,64,128]{2,0,1:T(4,128)} %copy.349), calls=%async_computation.5 | async-start | bytes 262144 | tf_op jit(solution)/shard_map/all_to_all | solution.py:37
  138.8 16.9 %all-to-all-start.6 = ((f32[128,2,128]{2,1,0:T(2,128)}), f32[128,2,128]{2,1,0:T(2,128)S(1)}, u32[]{:S(2)}, u32[]{:S(2)}) async-start(f32[128,2,128]{2,1,0:T(2,128)} %copy.359), calls=%async_computation.6 | async-start | bytes 262144 | tf_op jit(solution)/shard_map/all_to_all | solution.py:33
  142.8 0.7 copy-start.8
  157.2 3.9 copy-start.7
  157.2 4.0 copy-start.3
  157.2 16.3 %all-to-all-start.7 = ((f32[32,1,256]{2,1,0:T(1,128)}), f32[32,1,256]{2,1,0:T(1,128)S(1)}, u32[]{:S(2)}, u32[]{:S(2)}) async-start(f32[32,1,256]{2,1,0:T(1,128)} %reshape.522), calls=%async_computation.7 | async-start | bytes 65536 | tf_op jit(solution)/shard_map/all_to_all | solution.py:37
  175.2 8.2 %copy-start.1 = (f32[25426]{0:T(1024)S(1)}, f32[25426]{0:T(1024)}, u32[]{:S(2)}) copy-start(f32[25426]{0:T(1024)} %param.19) | copy-start | bytes 305116
  175.2 16.3 %all-to-all-start.8 = ((bf16[16,128,64]{1,2,0:T(8,128)(2,1)}), bf16[16,128,64]{1,2,0:T(8,128)(2,1)S(1)}, u32[]{:S(2)}, u32[]{:S(2)}) async-start(bf16[16,128,64]{1,2,0:T(8,128)(2,1)} %stack.2), calls=%async_computation.8 | async-start | bytes 524288 | tf_op jit(solution)/shard_map/all_to_all | solution.py:143
  183.3 82.3 %reduce-scatter.7.cloned.1.call-start = ((), (), s32[]{:S(2)}) async-start(), calls=%async_computation.20 | async-start | bytes 557056
  183.4 8.1 %copy-start.4 = (bf16[128,64]{0,1:T(8,128)(2,1)S(1)}, bf16[128,64]{0,1:T(8,128)(2,1)}, u32[]{:S(2)}) copy-start(bf16[128,64]{0,1:T(8,128)(2,1)} %param.15) | copy-start | bytes 49156
  292.1 16.9 %all-to-all-start.10 = ((f32[4,64,128]{2,0,1:T(4,128)}), f32[4,64,128]{2,0,1:T(4,128)S(1)}, u32[]{:S(2)}, u32[]{:S(2)}) async-start(f32[4,64,128]{2,0,1:T(4,128)} %copy.366), calls=%async_computation.10 | async-start | bytes 262144 | tf_op jit(solution)/shard_map/all_to_all | solution.py:37
  367.4 16.9 %all-to-all-start.14 = ((f32[4,64,128]{2,0,1:T(4,128)}), f32[4,64,128]{2,0,1:T(4,128)S(1)}, u32[]{:S(2)}, u32[]{:S(2)}) async-start(f32[4,64,128]{2,0,1:T(4,128)} %copy.381), calls=%async_computation.14 | async-start | bytes 262144 | tf_op jit(solution)/shard_map/all_to_all | solution.py:37
  388.2 18.3 %all-to-all-start.15 = ((f32[128,2,130]{2,1,0:T(2,128)}), f32[128,2,130]{2,1,0:T(2,128)S(1)}, u32[]{:S(2)}, u32[]{:S(2)}) async-start(f32[128,2,130]{2,1,0:T(2,128)} %copy.387), calls=%async_computation.15 | async-start | bytes 524288 | tf_op jit(solution)/shard_map/all_to_all | solution.py:33
  392.1 137.8 %reduce-scatter.5.cloned.1.call-start = ((), (), s32[]{:S(2)}) async-start(), calls=%async_computation.19 | async-start | bytes 540672 | tf_op jit(solution)/shard_map/reduce_scatter | solution.py:150
  408.0 17.6 %all-to-all-start.16 = ((f32[4,32,65]{2,0,1:T(4,128)}), f32[4,32,65]{2,0,1:T(4,128)S(1)}, u32[]{:S(2)}, u32[]{:S(2)}) async-start(f32[4,32,65]{2,0,1:T(4,128)} %copy.389), calls=%async_computation.16 | async-start | bytes 131072 | tf_op jit(solution)/shard_map/all_to_all | solution.py:37
Sparse Core Ops, SparseCore 0:
  193.1 72.4 reduce-scatter.6
Sparse Core Ops, SparseCore 1:
  398.4 131.4 reduce-scatter.4
